TPU v7x, 128 devices: a whole 4x4x4 slice. The times are simulated.
128 devices in a mesh: req: 32 (over z, x, core), tp: 4 (over y).
Axes of the slice: x: 4, y: 4, z: 4, core: 2. Of those that a mesh axis runs over, the one named last changes fastest.
Arguments:
- tokens: bfloat16 [16384, 2560], P('req'), may hold values from -6 to 6
- lengths: int32 [32], P('req'), may hold values from 1 to 512, as said below
- page_slot: int32 [128], replicated, may hold values from 0 to 127, as said below
- trainer_layout: int32 [128], replicated, may hold values from 0 to 127, each once
- trainer_qkv: float32 [2560, 3840], P(('req', 'tp'))
- trainer_gateup: float32 [2560, 13824], P(('req', 'tp')), may hold values from -0.125 to 0.125
- attn_gain: float32 [2560], replicated, may hold values from 0.1 to 1.9
- ffn_gain: float32 [2560], replicated, may hold values from 0.1 to 1.9
- out_proj: bfloat16 [2560, 2560], P('tp'), may hold values from -0.125 to 0.125
- down_proj: bfloat16 [6912, 2560], P('tp'), may hold values from -0.078125 to 0.078125
Outputs:
- layer_out: bfloat16 [16384, 2560], P(('req', 'tp'))
- kv_cache: bfloat16 [128, 128, 1280], P('req', None, 'tp')
Inputs may be any that keep to these rules, and one draw needn't show every extreme that they name: `lengths`: heavy-tailed; some request has exactly 512. `page_slot`: a permutation; pool slot s belongs to request device s // 4; the 4 pages of one request belong to 4 different devices. `trainer_layout`: a permutation; shard s is the trainer shard on the device with index s over req and tp together.
All inputs are finite; a program needn't handle non-finite values.
Results may differ from a plain program's by a relative error of at most 0.0065.
The roundings to bfloat16 on the way count: a program that leaves them out, or rounds other values in their place, can miss the bound.
Values may be sent and summed in bfloat16 or wider, within the bound.
A program may use at most 192 MiB of HBM per device.

v0:
```python
import jax
import jax.numpy as jnp
from jax import lax
from jax.sharding import PartitionSpec as P

HD = 80
PAGE = 128
eps_norm = 1e-05
theta_base = 10000.0


def normed(values, gain):
    scale = lax.rsqrt(jnp.mean(values * values, axis=-1, keepdims=True) + eps_norm)
    return (values * scale * gain).astype(jnp.bfloat16)


def rotary(field, head_dim):
    half = head_dim // 2
    count = field.shape[0]
    freq = theta_base ** (-jnp.arange(half, dtype=jnp.float32) * 2.0 / head_dim)
    angles = jnp.arange(count, dtype=jnp.float32)[:, None] * freq[None, :]
    cosine = jnp.cos(angles)[:, None, :]
    sine = jnp.sin(angles)[:, None, :]
    first = field[..., :half]
    second = field[..., half:]
    return jnp.concatenate(
        [first * cosine - second * sine, second * cosine + first * sine], axis=-1
    )


def body(
    tokens,
    lengths,
    page_slot,
    trainer_layout,
    trainer_qkv,
    trainer_gateup,
    attn_gain,
    ffn_gain,
    out_proj,
    down_proj,
):
    n_tp = lax.axis_size("tp")
    n_req = lax.axis_size("req")
    devices = n_tp * n_req
    rows_each = trainer_qkv.shape[0]
    seq_len = tokens.shape[0]
    model_dim = tokens.shape[1]
    head_dim = HD
    local_heads = out_proj.shape[0] // head_dim
    group_cols = trainer_qkv.shape[1] // n_tp
    local_kv = (group_cols // head_dim - local_heads) // 2
    group = local_heads // local_kv
    q_cols = local_heads * head_dim
    k_cols = local_kv * head_dim
    ff_local = down_proj.shape[0]
    qkv_half, gu_half = (
        lax.all_to_all(
            trainer_qkv.astype(jnp.bfloat16), "tp", split_axis=1, concat_axis=0, tiled=True
        ),
        lax.all_to_all(
            trainer_gateup.astype(jnp.bfloat16), "tp", split_axis=1, concat_axis=0, tiled=True
        ),
    )
    x_f = tokens.astype(jnp.float32)
    x_norm = normed(x_f, attn_gain)
    row_of = (trainer_layout[:, None] * rows_each + jnp.arange(rows_each, dtype=jnp.int32)).reshape(
        1, -1
    )
    place = (jnp.arange(model_dim, dtype=jnp.int32)[:, None] == row_of).astype(jnp.bfloat16)
    x_norm = jnp.dot(x_norm, place, preferred_element_type=jnp.float32).astype(jnp.bfloat16)
    qkv_weight = lax.all_gather(qkv_half, "req", axis=0, tiled=True)
    gu_weight = lax.all_gather(gu_half, "req", axis=0, tiled=True)
    joined = jnp.dot(x_norm, qkv_weight, preferred_element_type=jnp.float32)
    query = rotary(joined[:, :q_cols].reshape(seq_len, local_heads, head_dim), head_dim)
    keys = rotary(
        joined[:, q_cols : q_cols + k_cols].reshape(seq_len, local_kv, head_dim), head_dim
    )
    query16 = query.astype(jnp.bfloat16).reshape(seq_len, local_kv, group, head_dim)
    keys16 = keys.astype(jnp.bfloat16)
    values16 = (
        joined[:, q_cols + k_cols :].reshape(seq_len, local_kv, head_dim).astype(jnp.bfloat16)
    )
    scores = jnp.einsum(
        "qkgd,skd->kgqs", query16, keys16, preferred_element_type=jnp.float32
    ) * head_dim ** (-0.5)
    slots = jnp.arange(seq_len, dtype=jnp.int32)
    length = lengths[0]
    allowed = (slots[None, :] <= slots[:, None]) & (slots[None, :] < length)
    scores = jnp.where(allowed[None, None], scores, -1e30)
    probs = jax.nn.softmax(scores, axis=-1).astype(jnp.bfloat16)
    context = jnp.einsum(
        "kgqs,skd->qkgd", probs, values16, preferred_element_type=jnp.float32
    ).astype(jnp.bfloat16)
    partial_out = jnp.dot(
        context.reshape(seq_len, q_cols), out_proj, preferred_element_type=jnp.float32
    )
    share = seq_len // n_tp
    tp_index = lax.axis_index("tp")
    mixed = lax.psum_scatter(
        partial_out.astype(jnp.bfloat16), "tp", scatter_dimension=0, tiled=True
    )
    x_share = lax.dynamic_slice_in_dim(tokens, tp_index * share, share, 0)
    resid_share = x_share.astype(jnp.float32) + mixed.astype(jnp.float32)
    h_share = normed(resid_share, ffn_gain)
    h_share = jnp.dot(h_share, place, preferred_element_type=jnp.float32).astype(jnp.bfloat16)
    h_norm = lax.all_gather(h_share, "tp", axis=0, tiled=True)
    projected = jnp.dot(h_norm, gu_weight, preferred_element_type=jnp.float32)
    hidden = (jax.nn.silu(projected[:, :ff_local]) * projected[:, ff_local:]).astype(jnp.bfloat16)
    down = jnp.dot(hidden, down_proj, preferred_element_type=jnp.float32)
    added = lax.psum_scatter(
        down.astype(jnp.bfloat16), "tp", scatter_dimension=0, tiled=True
    ).astype(jnp.float32)
    share_slots = tp_index * share + jnp.arange(share, dtype=jnp.int32)
    live_share = (share_slots < length).astype(jnp.float32)
    layer_out = ((resid_share + added) * live_share[:, None]).astype(jnp.bfloat16)
    live_rows = (slots < length)[:, None]
    key_rows = keys16.reshape(seq_len, k_cols)
    value_rows = values16.reshape(seq_len, k_cols)
    cache_rows = jnp.concatenate(
        [
            jnp.where(live_rows, key_rows, jnp.zeros_like(key_rows)),
            jnp.where(live_rows, value_rows, jnp.zeros_like(value_rows)),
        ],
        axis=1,
    )
    pages = cache_rows.reshape(seq_len // PAGE, PAGE, 2 * k_cols)
    pool_size = pages.shape[0]
    owner = lax.axis_index("req")
    targets = owner * pool_size + jnp.arange(pool_size, dtype=jnp.int32)
    picks = (page_slot[:, None] == targets[None, :]).astype(jnp.bfloat16)
    pool = jnp.einsum(
        "np,nsc->psc",
        picks,
        lax.all_gather(pages, "req", axis=0, tiled=True),
        preferred_element_type=jnp.float32,
    )
    kv_cache = pool.astype(jnp.bfloat16)
    return (layer_out, kv_cache)


def solution(mesh):
    return jax.shard_map(
        body,
        mesh=mesh,
        in_specs=(
            P("req", None),
            P("req"),
            P(),
            P(),
            P(("req", "tp"), None),
            P(("req", "tp"), None),
            P(),
            P(),
            P("tp", None),
            P("tp", None),
        ),
        out_specs=(P(("req", "tp"), None), P("req", None, "tp")),
        check_vma=False,
    )
```

profile of v0, /device:TPU:1, one launch (start us, length us, event | category | flops | bytes accessed | tf_op | source)
XLA Modules:
  0.0 364.6 jit_solution(9727156666313900420)
XLA Ops:
  7.2 0.0 all-gather.5.cloned.1.call-start
  7.2 1.2 convert_element_type.84
  8.4 0.9 all_to_all.28
  9.3 1.0 copy.18
  10.3 10.0 %all_to_all.38 = bf16[20,4,960]{2,0,1:T(8,128)(2,1)S(1)} all-to-all(bf16[20,4,960]{2,0,1:T(8,128)(2,1)S(1)} %copy.18), channel_id=1, replica_groups=mesh['req'=32,'tp'=4] {'tp'}, dimensions={1} | all-to-all | bytes 307200 | tf_op jit(solution)/shard_map/all_to_all | solution.py:58
  20.3 0.7 all_to_all.31
  21.0 0.0 all-gather.5.cloned.1.call-update
  21.0 0.0 reduce-scatter.3.cloned.1.call-start
  21.7 0.7 broadcast_multiply_fusion
  22.4 0.1 iota_add_fusion
  22.5 0.1 add.92
  22.6 2.3 fusion.8
  24.9 0.4 fusion.39
  25.3 0.9 fusion.27
  26.2 44.8 %all-gather.5.cloned.1.call-done = bf16[2560,960]{1,0:T(8,128)(2,1)} async-done(((bf16[80,960]{1,0:T(8,128)(2,1)}), bf16[2560,960]{1,0:T(8,128)(2,1)}) %all-gather.5.cloned.1.call-update) | async-done | bytes 4915216 | tf_op jit(solution)/shard_map/all_gather | solution.py:72
  70.9 14.3 %fusion.57 = f32[512,960]{0,1:T(8,128)} fusion(bf16[2560,960]{1,0:T(8,128)(2,1)} %all-gather.5.cloned.1.call-done, s32[2560]{0:T(1024)S(1)} %add.92, bf16[512,2560]{1,0:T(8,128)(2,1)} %param.10, f32[2560]{0:T(1024)S(1)} %copy-done.7, f32[512]{0:T(512)S(1)} %add_rsqrt_fusion), kind=kOutput, calls=%fused_computation.79 | convolution fusion | flops 9240576000 | bytes 9525248 | tf_op jit(solution)/shard_map/dot_general | solution.py:74
  85.2 1.8 select_bitcast_fusion
  87.1 1.0 subtract_convert_fusion
  88.1 0.7 multiply_subtract_fusion
  88.8 7.8 %fusion.52 = (f32[2,4,512]{2,1,0:T(4,128)S(1)}, f32[2,4,512,512]{2,3,1,0:T(8,128)}) fusion(pred[512,512]{0,1:T(8,128)(4,1)} %fusion.27, bf16[512,2,4,40]{0,3,2,1:T(8,128)(2,1)} %bitcast.67, bf16[512,2,4,40]{0,3,2,1:T(8,128)(2,1)} %bitcast.66, bf16[512,2,40]{0,2,1:T(8,128)(2,1)} %get-tuple-element.13, bf16[512,2,40]{0,2,1:T(8,128)(2,1)S(1)} %get-tuple-element.12), kind=kOutput, calls=%fused_computation.78 | convolution fusion | flops 345571840 | bytes 9486336 | tf_op jit(solution)/shard_map/sub | solution.py:91
  96.6 4.2 %fusion.23 = bf16[2,80,4,512]{3,1,2,0:T(8,128)(2,1)S(1)} fusion(bf16[512,2,80,1]{0,2,3,1:T(8,128)(2,1)S(1)} %bitcast.68, f32[2,4,512,512]{2,3,1,0:T(8,128)} %get-tuple-element.17, f32[2,4,512]{2,1,0:T(4,128)S(1)} %get-tuple-element.16), kind=kOutput, calls=%fused_computation.30 | convolution fusion | flops 340066304 | bytes 9224192 | tf_op jit(solution)/shard_map/kgqs,skd->qkgd/dot_general | solution.py:92
  100.8 3.8 %convolution_convert_fusion.1 = bf16[512,2560]{1,0:T(8,128)(2,1)} fusion(bf16[512,640]{0,1:T(8,128)(2,1)S(1)} %bitcast.64, bf16[640,2560]{1,0:T(8,128)(2,1)S(1)} %copy-done), kind=kOutput, calls=%fused_computation.19 | convolution fusion | flops 1679032320 | bytes 6553600 | tf_op jit(solution)/shard_map/dot_general | solution.py:95
  104.6 0.0 reduce-scatter.3.cloned.1.call-update
  104.6 0.0 all-gather.7.cloned.1.call-start
  104.7 33.0 %reduce-scatter.3.cloned.1.call-done = bf16[128,2560]{1,0:T(8,128)(2,1)} async-done(((bf16[512,2560]{1,0:T(8,128)(2,1)}), bf16[128,2560]{1,0:T(8,128)(2,1)}) %reduce-scatter.3.cloned.1.call-update) | async-done | bytes 655376 | tf_op jit(solution)/shard_map/reduce_scatter | solution.py:100
  137.7 1.6 multiply_reduce_fusion
  139.3 8.0 %fusion.17 = bf16[128,2560]{1,0:T(8,128)(2,1)} fusion(s32[2560]{0:T(1024)S(1)} %add.92, bf16[128,2560]{1,0:T(8,128)(2,1)} %reduce-scatter.3.cloned.1.call-done, f32[2560]{0:T(1024)S(1)} %copy-done.8, f32[128]{0:T(128)S(1)} %add_rsqrt_fusion.1, bf16[512,2560]{1,0:T(8,128)(2,1)} %param.10, s32[]{:T(128)S(6)} %select_n.15), kind=kOutput, calls=%fused_computation.26 | convolution fusion | flops 1686568960 | bytes 1987076 | tf_op jit(solution)/shard_map/dot_general | solution.py:106
  147.3 0.0 all-gather.7.cloned.1.call-update
  147.3 0.0 all-gather.9.cloned.1.call-start
  147.4 0.1 convert_element_type.95
  147.5 0.2 all_to_all.32
  147.7 0.1 copy.20
  147.8 12.4 %all_to_all.39 = bf16[20,4,3456]{2,0,1:T(8,128)(2,1)S(1)} all-to-all(bf16[20,4,3456]{2,0,1:T(8,128)(2,1)S(1)} %copy.20), channel_id=1, replica_groups=mesh['req'=32,'tp'=4] {'tp'}, dimensions={1} | all-to-all | bytes 1105920 | tf_op jit(solution)/shard_map/all_to_all | solution.py:61
  160.2 0.9 all_to_all.35
  161.1 0.0 all-gather.9.cloned.1.call-update
  161.2 0.0 all-gather.11.cloned.1.call-start
  161.4 0.7 pad_maximum_fusion.7
  162.2 0.3 reduce-scatter.5.cloned.1.call-start
  162.4 20.4 %all-gather.7.cloned.1.call-done = bf16[512,2560]{1,0:T(8,128)(2,1)} async-done(((bf16[128,2560]{1,0:T(8,128)(2,1)}), bf16[512,2560]{1,0:T(8,128)(2,1)}) %all-gather.7.cloned.1.call-update) | async-done | bytes 2621456 | tf_op jit(solution)/shard_map/all_gather | solution.py:107
  182.9 76.9 %all-gather.9.cloned.1.call-done = bf16[2560,3456]{1,0:T(8,128)(2,1)} async-done(((bf16[80,3456]{1,0:T(8,128)(2,1)}), bf16[2560,3456]{1,0:T(8,128)(2,1)}) %all-gather.9.cloned.1.call-update) | async-done | bytes 17694736 | tf_op jit(solution)/shard_map/all_gather | solution.py:73
  259.8 14.5 %fusion.58 = f32[512,3456]{1,0:T(8,128)S(1)} fusion(bf16[512,2560]{1,0:T(8,128)(2,1)} %all-gather.7.cloned.1.call-done, bf16[2560,3456]{1,0:T(8,128)(2,1)} %all-gather.9.cloned.1.call-done), kind=kOutput, calls=%fused_computation.80 | convolution fusion | flops 9059696640 | bytes 27394048 | tf_op jit(solution)/shard_map/dot_general | solution.py:108
  274.3 10.0 %convolution_convert_fusion = bf16[512,2560]{1,0:T(8,128)(2,1)} fusion(bf16[1728,2560]{1,0:T(8,128)(2,1)} %param.19, f32[512,3456]{1,0:T(8,128)S(1)} %fusion.58), kind=kOutput, calls=%fused_computation.18 | convolution fusion | flops 4536467456 | bytes 18808832 | tf_op jit(solution)/shard_map/dot_general | solution.py:110
  284.3 0.0 reduce-scatter.5.cloned.1.call-update
  284.4 35.4 %all-gather.11.cloned.1.call-done = bf16[128,128,320]{1,2,0:T(8,128)(2,1)} async-done(((bf16[4,128,320]{1,2,0:T(8,128)(2,1)}), bf16[128,128,320]{1,2,0:T(8,128)(2,1)}) %all-gather.11.cloned.1.call-update) | async-done | bytes 10485776 | tf_op jit(solution)/shard_map/all_gather | solution.py:135
  319.8 9.8 %fusion.24 = bf16[4,128,320]{1,0,2:T(4,128)(2,1)S(1)} fusion(bf16[128,128,320]{1,2,0:T(8,128)(2,1)} %all-gather.11.cloned.1.call-done, s32[128]{0:T(128)S(1)} %copy-done.6, s32[4]{0:T(128)S(1)} %iota_add_fusion.1), kind=kOutput, calls=%fused_computation.35 | convolution fusion | flops 42107392 | bytes 10813968 | tf_op jit(solution)/shard_map/np,nsc->psc/dot_general | solution.py:132
  329.6 0.8 copy.24
  330.3 24.9 %reduce-scatter.5.cloned.1.call-done = bf16[128,2560]{1,0:T(8,128)(2,1)} async-done(((bf16[512,2560]{1,0:T(8,128)(2,1)}), bf16[128,2560]{1,0:T(8,128)(2,1)}) %reduce-scatter.5.cloned.1.call-update) | async-done | bytes 655376 | tf_op jit(solution)/shard_map/reduce_scatter | solution.py:111
  355.2 2.6 multiply_convert_fusion
  (34 shorter events, 0.2 us)
Async XLA Ops:
  7.2 93.7 %copy-start = (bf16[640,2560]{1,0:T(8,128)(2,1)S(1)}, bf16[640,2560]{1,0:T(8,128)(2,1)}, u32[]{:S(2)}) copy-start(bf16[640,2560]{1,0:T(8,128)(2,1)} %param.18) | copy-start | bytes 9830404
  7.2 63.8 %copy-start.7 = (f32[2560]{0:T(1024)S(1)}, f32[2560]{0:T(1024)}, u32[]{:S(2)}) copy-start(f32[2560]{0:T(1024)} %param.16) | copy-start | bytes 30724
  7.2 63.7 %all-gather.5.cloned.1.call-start = ((), (), s32[]{:S(2)}) async-start(), calls=%async_computation.4 | async-start | bytes 5406720 | tf_op jit(solution)/shard_map/all_gather | solution.py:72
  21.0 116.7 %reduce-scatter.3.cloned.1.call-start = ((), (), s32[]{:S(2)}) async-start(), calls=%async_computation.5 | async-start | bytes 3276800 | tf_op jit(solution)/shard_map/reduce_scatter | solution.py:100
  85.2 1.9 slice-start.1
  85.2 2.9 slice-start
  88.8 7.8 %copy-start.5 = (bf16[512,160]{0,1:T(8,128)(2,1)S(1)}, bf16[512,160]{0,1:T(8,128)(2,1)}, u32[]{:S(2)}) copy-start(bf16[512,160]{0,1:T(8,128)(2,1)} %get-tuple-element.9) | copy-start | bytes 491524
  100.8 38.5 %copy-start.8 = (f32[2560]{0:T(1024)S(1)}, f32[2560]{0:T(1024)}, u32[]{:S(2)}) copy-start(f32[2560]{0:T(1024)} %param.17) | copy-start | bytes 30724
  104.6 78.2 %all-gather.7.cloned.1.call-start = ((), (), s32[]{:S(2)}) async-start(), calls=%async_computation.6 | async-start | bytes 3276800 | tf_op jit(solution)/shard_map/all_gather | solution.py:107
  139.3 8.1 %copy-start.2 = (f32[20,13824]{1,0:T(8,128)S(1)}, f32[20,13824]{1,0:T(8,128)}, u32[]{:S(2)}) copy-start(f32[20,13824]{1,0:T(8,128)} %param.15) | copy-start | bytes 3317764
  147.3 13.9 %copy-start.3 = (bf16[20,4,8,128]{3,2,1,0:T(8,128)(2,1)S(1)}, bf16[20,4,8,128]{3,2,1,0:T(8,128)(2,1)}, u32[]{:S(2)}) copy-start(bf16[20,4,8,128]{3,2,1,0:T(8,128)(2,1)} %get-tuple-element.8) | copy-start | bytes 491524
  147.3 14.0 %copy-start.4 = (bf16[512,2,40]{0,2,1:T(8,128)(2,1)S(1)}, bf16[512,2,40]{0,2,1:T(8,128)(2,1)}, u32[]{:S(2)}) copy-start(bf16[512,2,40]{0,2,1:T(8,128)(2,1)} %get-tuple-element.13) | copy-start | bytes 245764
  147.3 112.5 %all-gather.9.cloned.1.call-start = ((), (), s32[]{:S(2)}) async-start(), calls=%async_computation.7 | async-start | bytes 18247680 | tf_op jit(solution)/shard_map/all_gather | solution.py:73
  161.2 158.6 %all-gather.11.cloned.1.call-start = ((), (), s32[]{:S(2)}) async-start(), calls=%async_computation.9 | async-start | bytes 10813440 | tf_op jit(solution)/shard_map/all_gather | solution.py:135
  162.2 193.0 %reduce-scatter.5.cloned.1.call-start = ((), (), s32[]{:S(2)}) async-start(), calls=%async_computation.8 | async-start | bytes 3276800 | tf_op jit(solution)/shard_map/reduce_scatter | solution.py:111
  274.3 45.5 %copy-start.6 = (s32[128]{0:T(128)S(1)}, s32[128]{0:T(128)}, u32[]{:S(2)}) copy-start(s32[128]{0:T(128)} %param.12) | copy-start | bytes 1540
  319.8 38.0 %copy-start.1 = (bf16[640,2560]{1,0:T(8,128)(2,1)S(1)}, bf16[640,2560]{1,0:T(8,128)(2,1)}, u32[]{:S(2)}) copy-start(bf16[640,2560]{1,0:T(8,128)(2,1)} %param.18) | copy-start | bytes 9830404
Sparse Core Ops, SparseCore 0:
  21.2 49.7 all-gather.4
  104.7 32.9 reduce-scatter.2
  147.4 35.3 all-gather.6
  185.0 74.6 all-gather.8
  262.5 57.3 all-gather.10
  322.1 33.0 reduce-scatter.4
where the time goes:
time: 365 us
  waiting for transfers between devices  236 us (65%)
  matrix products  72.3 us (20%)
  blocking collectives  22.4 us (6%)
  between operations  15 us (4%)
  other arithmetic  14.1 us (4%)
  local copies, waits for them, and re-layouts  4.84 us (1%)
    all_gather x1, waiting for transfers between devices, body(): gu_weight = lax.all_gather(gu_half, 'req', axis=0, tiled=True)  76.9 us
    all_gather x1, waiting for transfers between devices, body(): qkv_weight = lax.all_gather(qkv_half, 'req', axis=0, tiled=True)  44.8 us
    all_gather x1, waiting for transfers between devices, body(): lax.all_gather(pages, 'req', axis=0, tiled=True)  35.4 us
    reduce_scatter x1, waiting for transfers between devices, body(): lax.psum_scatter(partial_out.astype(jnp.bfloat16), 'tp', scatter_dimensio...  33 us
    reduce_scatter x1, waiting for transfers between devices, body(): lax.psum_scatter(down.astype(jnp.bfloat16), 'tp', scatter_dimension=0, ti...  24.9 us
    all_gather x1, waiting for transfers between devices, body(): h_norm = lax.all_gather(h_share, 'tp', axis=0, tiled=True)  20.4 us
    dot_general x1, matrix products, body(): projected = jnp.dot(h_norm, gu_weight, preferred_element_type=jnp.float32)  14.5 us
    dot_general x1, matrix products, body(): joined = jnp.dot(x_norm, qkv_weight, preferred_element_type=jnp.float32)  14.3 us
  transfers between devices with their start and end apart: 6, of which 6 were waited for; matrix products, arithmetic and copies ran while one was open for 11% of the time, Pallas kernels for 0%

commit v1 on v0

--- a/solution.py
+++ b/solution.py
@@ -69,7 +69,9 @@
     )
     place = (jnp.arange(model_dim, dtype=jnp.int32)[:, None] == row_of).astype(jnp.bfloat16)
     x_norm = jnp.dot(x_norm, place, preferred_element_type=jnp.float32).astype(jnp.bfloat16)
-    qkv_weight = lax.all_gather(qkv_half, "req", axis=0, tiled=True)
+    qkv_weight = jnp.concatenate(
+        lax.all_to_all(jnp.stack([qkv_half] * lax.axis_size("req")), "req", 0, 0), axis=0
+    )
     gu_weight = lax.all_gather(gu_half, "req", axis=0, tiled=True)
     joined = jnp.dot(x_norm, qkv_weight, preferred_element_type=jnp.float32)
     query = rotary(joined[:, :q_cols].reshape(seq_len, local_heads, head_dim), head_dim)

time: 365 us -> 391 us (1.071)
  waiting for transfers between devices: 236 us -> 248 us
  starting transfers between devices: 0.47 us -> 10.6 us
  local copies, waits for them, and re-layouts: 4.84 us -> 8.79 us
    all_to_all x0 -> x1, waiting for transfers between devices: none -> 57 us  [body(): lax.all_to_all(jnp.stack([qkv_half] * lax.axis_size('req')), 'req', 0, 0)]
    all_gather x1 -> x0, waiting for transfers between devices: 44.8 us -> none  [body(): qkv_weight = lax.all_gather(qkv_half, 'req', axis=0, tiled=True)]
    all_to_all x0 -> x1, starting transfers between devices: none -> 10.2 us  [body(): lax.all_to_all(jnp.stack([qkv_half] * lax.axis_size('req')), 'req', 0, 0)]
    another operation x0 -> x2, local copies, waits for them, and re-layouts: none -> 4.66 us  [body(): jnp.stack([qkv_half] * lax.axis_size('req'))]
  transfers between devices with their start and end apart: 6 -> 6, of which waited for: 6 -> 6; matrix products, arithmetic and copies ran while one was open for 11% -> 10% of each run, Pallas kernels for 0% -> 0%
where the time goes in v1:
time: 391 us; the launch traced here: 390 us
  waiting for transfers between devices  248 us (63%)
  matrix products  72.3 us (18%)
  blocking collectives  22.4 us (6%)
  between operations  14.7 us (4%)
  other arithmetic  13.4 us (3%)
  starting transfers between devices  10.6 us (3%)
  local copies, waits for them, and re-layouts  8.79 us (2%)
    all_gather x1, waiting for transfers between devices, body(): gu_weight = lax.all_gather(gu_half, 'req', axis=0, tiled=True)  77.1 us
    all_to_all x1, waiting for transfers between devices, body(): lax.all_to_all(jnp.stack([qkv_half] * lax.axis_size('req')), 'req', 0, 0)  57 us
    all_gather x1, waiting for transfers between devices, body(): lax.all_gather(pages, 'req', axis=0, tiled=True)  35.4 us
    reduce_scatter x1, waiting for transfers between devices, body(): lax.psum_scatter(partial_out.astype(jnp.bfloat16), 'tp', scatter_dimensio...  32.8 us
    reduce_scatter x1, waiting for transfers between devices, body(): lax.psum_scatter(down.astype(jnp.bfloat16), 'tp', scatter_dimension=0, ti...  24.9 us
    all_gather x1, waiting for transfers between devices, body(): h_norm = lax.all_gather(h_share, 'tp', axis=0, tiled=True)  20.5 us
    dot_general x1, matrix products, body(): projected = jnp.dot(h_norm, gu_weight, preferred_element_type=jnp.float32)  14.5 us
    dot_general x1, matrix products, body(): joined = jnp.dot(x_norm, qkv_weight, preferred_element_type=jnp.float32)  14.3 us
  transfers between devices with their start and end apart: 6, of which 6 were waited for; matrix products, arithmetic and copies ran while one was open for 10% of the time, Pallas kernels for 0%

profile of v1, /device:TPU:1, one launch (start us, length us, event | category | flops | bytes accessed | tf_op | source)
XLA Modules:
  0.0 390.0 jit_solution(16695766590954406069)
XLA Ops:
  7.2 1.2 convert_element_type.84
  8.3 0.9 all_to_all.29
  9.3 1.0 copy.18
  10.2 10.0 %all_to_all.40 = bf16[20,4,960]{2,0,1:T(8,128)(2,1)S(1)} all-to-all(bf16[20,4,960]{2,0,1:T(8,128)(2,1)S(1)} %copy.18), channel_id=1, replica_groups=mesh['req'=32,'tp'=4] {'tp'}, dimensions={1} | all-to-all | bytes 307200 | tf_op jit(solution)/shard_map/all_to_all | solution.py:58
  20.2 0.7 stack.4
  21.0 3.9 %stack.5 = bf16[32,80,960]{2,1,0:T(8,128)(2,1)} broadcast(bf16[80,960]{1,0:T(8,128)(2,1)} %stack.4), dimensions={1,2} | broadcast | bytes 5068800 | tf_op jit(solution)/shard_map/stack | solution.py:73
  24.9 10.2 %all-to-all-start.1 = ((bf16[32,80,960]{2,1,0:T(8,128)(2,1)}), bf16[32,80,960]{2,1,0:T(8,128)(2,1)}, u32[]{:S(2)}, u32[]{:S(2)}) async-start(bf16[32,80,960]{2,1,0:T(8,128)(2,1)} %stack.5), calls=%async_computation.1 | async-start | bytes 10485760 | tf_op jit(solution)/shard_map/all_to_all | solution.py:73
  35.1 0.0 reduce-scatter.3.cloned.1.call-start
  35.2 0.1 iota_add_fusion
  35.3 0.1 add.92
  36.1 2.3 fusion.8
  38.4 0.4 fusion.39
  38.8 0.9 fusion.27
  39.6 57.0 %all-to-all-done.1 = bf16[32,80,960]{2,1,0:T(8,128)(2,1)} async-done(((bf16[32,80,960]{2,1,0:T(8,128)(2,1)}), bf16[32,80,960]{2,1,0:T(8,128)(2,1)}, u32[]{:S(2)}, u32[]{:S(2)}) %all-to-all-start.1) | async-done | bytes 4915232 | tf_op jit(solution)/shard_map/all_to_all | solution.py:73
  96.6 14.3 %fusion.57 = f32[512,960]{0,1:T(8,128)} fusion(bf16[2560,960]{1,0:T(8,128)(2,1)} %bitcast.1, s32[2560]{0:T(1024)S(1)} %add.92, bf16[512,2560]{1,0:T(8,128)(2,1)} %param.10, f32[2560]{0:T(1024)S(1)} %copy-done.7, f32[512]{0:T(512)S(1)} %add_rsqrt_fusion), kind=kOutput, calls=%fused_computation.79 | convolution fusion | flops 9240576000 | bytes 9525248 | tf_op jit(solution)/shard_map/dot_general | solution.py:76
  110.9 1.9 select_bitcast_fusion
  112.8 0.7 multiply_subtract_fusion
  113.5 1.0 subtract_convert_fusion
  114.5 7.8 %fusion.52 = (f32[2,4,512]{2,1,0:T(4,128)S(1)}, f32[2,4,512,512]{2,3,1,0:T(8,128)}) fusion(pred[512,512]{0,1:T(8,128)(4,1)} %fusion.27, bf16[512,2,4,40]{0,3,2,1:T(8,128)(2,1)} %bitcast.68, bf16[512,2,4,40]{0,3,2,1:T(8,128)(2,1)} %bitcast.67, bf16[512,2,40]{0,2,1:T(8,128)(2,1)} %get-tuple-element.13, bf16[512,2,40]{0,2,1:T(8,128)(2,1)S(1)} %get-tuple-element.12), kind=kOutput, calls=%fused_computation.78 | convolution fusion | flops 345571840 | bytes 9486336 | tf_op jit(solution)/shard_map/sub | solution.py:93
  122.3 4.2 %fusion.23 = bf16[2,80,4,512]{3,1,2,0:T(8,128)(2,1)S(1)} fusion(bf16[512,2,80,1]{0,2,3,1:T(8,128)(2,1)S(1)} %bitcast.69, f32[2,4,512,512]{2,3,1,0:T(8,128)} %get-tuple-element.17, f32[2,4,512]{2,1,0:T(4,128)S(1)} %get-tuple-element.16), kind=kOutput, calls=%fused_computation.30 | convolution fusion | flops 340066304 | bytes 9224192 | tf_op jit(solution)/shard_map/kgqs,skd->qkgd/dot_general | solution.py:94
  126.5 3.8 convolution_convert_fusion.1
  130.3 0.0 reduce-scatter.3.cloned.1.call-update
  130.3 0.0 all-gather.4.cloned.1.call-start
  130.4 32.8 %reduce-scatter.3.cloned.1.call-done = bf16[128,2560]{1,0:T(8,128)(2,1)} async-done(((bf16[512,2560]{1,0:T(8,128)(2,1)}), bf16[128,2560]{1,0:T(8,128)(2,1)}) %reduce-scatter.3.cloned.1.call-update) | async-done | bytes 655376 | tf_op jit(solution)/shard_map/reduce_scatter | solution.py:102
  163.2 1.6 multiply_reduce_fusion
  164.8 8.0 %fusion.17 = bf16[128,2560]{1,0:T(8,128)(2,1)} fusion(s32[2560]{0:T(1024)S(1)} %add.92, bf16[128,2560]{1,0:T(8,128)(2,1)} %reduce-scatter.3.cloned.1.call-done, f32[2560]{0:T(1024)S(1)} %copy-done.8, f32[128]{0:T(128)S(1)} %add_rsqrt_fusion.1, bf16[512,2560]{1,0:T(8,128)(2,1)} %param.10, s32[]{:T(128)S(6)} %select_n.15), kind=kOutput, calls=%fused_computation.26 | convolution fusion | flops 1686568960 | bytes 1987076 | tf_op jit(solution)/shard_map/dot_general | solution.py:108
  172.8 0.0 all-gather.4.cloned.1.call-update
  172.8 0.0 all-gather.6.cloned.1.call-start
  172.9 0.1 convert_element_type.95
  172.9 0.2 all_to_all.33
  173.2 0.1 copy.20
  173.3 12.4 %all_to_all.41 = bf16[20,4,3456]{2,0,1:T(8,128)(2,1)S(1)} all-to-all(bf16[20,4,3456]{2,0,1:T(8,128)(2,1)S(1)} %copy.20), channel_id=1, replica_groups=mesh['req'=32,'tp'=4] {'tp'}, dimensions={1} | all-to-all | bytes 1105920 | tf_op jit(solution)/shard_map/all_to_all | solution.py:61
  185.7 0.9 all_to_all.36
  186.6 0.0 all-gather.6.cloned.1.call-update
  186.6 0.0 all-gather.8.cloned.1.call-start
  186.9 0.7 pad_maximum_fusion.7
  187.6 0.0 all-gather.8.cloned.1.call-update
  187.6 0.3 reduce-scatter.5.cloned.1.call-start
  187.9 20.5 %all-gather.4.cloned.1.call-done = bf16[512,2560]{1,0:T(8,128)(2,1)} async-done(((bf16[128,2560]{1,0:T(8,128)(2,1)}), bf16[512,2560]{1,0:T(8,128)(2,1)}) %all-gather.4.cloned.1.call-update) | async-done | bytes 2621456 | tf_op jit(solution)/shard_map/all_gather | solution.py:109
  208.4 77.1 %all-gather.6.cloned.1.call-done = bf16[2560,3456]{1,0:T(8,128)(2,1)} async-done(((bf16[80,3456]{1,0:T(8,128)(2,1)}), bf16[2560,3456]{1,0:T(8,128)(2,1)}) %all-gather.6.cloned.1.call-update) | async-done | bytes 17694736 | tf_op jit(solution)/shard_map/all_gather | solution.py:75
  285.4 14.5 %fusion.58 = f32[512,3456]{1,0:T(8,128)S(1)} fusion(bf16[512,2560]{1,0:T(8,128)(2,1)} %all-gather.4.cloned.1.call-done, bf16[2560,3456]{1,0:T(8,128)(2,1)} %all-gather.6.cloned.1.call-done), kind=kOutput, calls=%fused_computation.80 | convolution fusion | flops 9059696640 | bytes 27394048 | tf_op jit(solution)/shard_map/dot_general | solution.py:110
  300.0 10.0 %convolution_convert_fusion = bf16[512,2560]{1,0:T(8,128)(2,1)} fusion(bf16[1728,2560]{1,0:T(8,128)(2,1)} %param.19, f32[512,3456]{1,0:T(8,128)S(1)} %fusion.58), kind=kOutput, calls=%fused_computation.18 | convolution fusion | flops 4536467456 | bytes 18808832 | tf_op jit(solution)/shard_map/dot_general | solution.py:112
  310.0 0.0 reduce-scatter.5.cloned.1.call-update
  310.0 35.4 %all-gather.8.cloned.1.call-done = bf16[128,128,320]{1,2,0:T(8,128)(2,1)} async-done(((bf16[4,128,320]{1,2,0:T(8,128)(2,1)}), bf16[128,128,320]{1,2,0:T(8,128)(2,1)}) %all-gather.8.cloned.1.call-update) | async-done | bytes 10485776 | tf_op jit(solution)/shard_map/all_gather | solution.py:137
  345.5 9.8 %fusion.24 = bf16[4,128,320]{1,0,2:T(4,128)(2,1)S(1)} fusion(bf16[128,128,320]{1,2,0:T(8,128)(2,1)} %all-gather.8.cloned.1.call-done, s32[128]{0:T(128)S(1)} %copy-done.6, s32[4]{0:T(128)S(1)} %iota_add_fusion.1), kind=kOutput, calls=%fused_computation.35 | convolution fusion | flops 42107392 | bytes 10813968 | tf_op jit(solution)/shard_map/np,nsc->psc/dot_general | solution.py:134
  355.2 0.8 copy.24
  356.0 24.9 %reduce-scatter.5.cloned.1.call-done = bf16[128,2560]{1,0:T(8,128)(2,1)} async-done(((bf16[512,2560]{1,0:T(8,128)(2,1)}), bf16[128,2560]{1,0:T(8,128)(2,1)}) %reduce-scatter.5.cloned.1.call-update) | async-done | bytes 655376 | tf_op jit(solution)/shard_map/reduce_scatter | solution.py:113
  380.9 2.6 multiply_convert_fusion
  (36 shorter events, 0.2 us)
Async XLA Ops:
  7.2 119.4 %copy-start = (bf16[640,2560]{1,0:T(8,128)(2,1)S(1)}, bf16[640,2560]{1,0:T(8,128)(2,1)}, u32[]{:S(2)}) copy-start(bf16[640,2560]{1,0:T(8,128)(2,1)} %param.18) | copy-start | bytes 9830404
  24.9 10.3 %copy-start.9 = (s32[128]{0:T(128)S(1)}, s32[128]{0:T(128)}, u32[]{:S(2)}) copy-start(s32[128]{0:T(128)} %param.13) | copy-start | bytes 1540
  24.9 71.7 %copy-start.7 = (f32[2560]{0:T(1024)S(1)}, f32[2560]{0:T(1024)}, u32[]{:S(2)}) copy-start(f32[2560]{0:T(1024)} %param.16) | copy-start | bytes 30724
  24.9 71.7 %all-to-all-start.1 = ((bf16[32,80,960]{2,1,0:T(8,128)(2,1)}), bf16[32,80,960]{2,1,0:T(8,128)(2,1)}, u32[]{:S(2)}, u32[]{:S(2)}) async-start(bf16[32,80,960]{2,1,0:T(8,128)(2,1)} %stack.5), calls=%async_computation.1 | async-start | bytes 10485760 | tf_op jit(solution)/shard_map/all_to_all | solution.py:73
  35.1 128.1 %reduce-scatter.3.cloned.1.call-start = ((), (), s32[]{:S(2)}) async-start(), calls=%async_computation.5 | async-start | bytes 3276800 | tf_op jit(solution)/shard_map/reduce_scatter | solution.py:102
  110.9 1.9 slice-start
  110.9 2.5 slice-start.1
  114.5 7.8 %copy-start.5 = (bf16[512,160]{0,1:T(8,128)(2,1)S(1)}, bf16[512,160]{0,1:T(8,128)(2,1)}, u32[]{:S(2)}) copy-start(bf16[512,160]{0,1:T(8,128)(2,1)} %get-tuple-element.9) | copy-start | bytes 491524
  126.5 38.2 %copy-start.8 = (f32[2560]{0:T(1024)S(1)}, f32[2560]{0:T(1024)}, u32[]{:S(2)}) copy-start(f32[2560]{0:T(1024)} %param.17) | copy-start | bytes 30724
  130.3 78.1 %all-gather.4.cloned.1.call-start = ((), (), s32[]{:S(2)}) async-start(), calls=%async_computation.6 | async-start | bytes 3276800 | tf_op jit(solution)/shard_map/all_gather | solution.py:109
  164.8 8.1 %copy-start.2 = (f32[20,13824]{1,0:T(8,128)S(1)}, f32[20,13824]{1,0:T(8,128)}, u32[]{:S(2)}) copy-start(f32[20,13824]{1,0:T(8,128)} %param.15) | copy-start | bytes 3317764
  172.8 13.9 %copy-start.4 = (bf16[512,2,40]{0,2,1:T(8,128)(2,1)S(1)}, bf16[512,2,40]{0,2,1:T(8,128)(2,1)}, u32[]{:S(2)}) copy-start(bf16[512,2,40]{0,2,1:T(8,128)(2,1)} %get-tuple-element.13) | copy-start | bytes 245764
  172.8 14.0 %copy-start.3 = (bf16[20,4,8,128]{3,2,1,0:T(8,128)(2,1)S(1)}, bf16[20,4,8,128]{3,2,1,0:T(8,128)(2,1)}, u32[]{:S(2)}) copy-start(bf16[20,4,8,128]{3,2,1,0:T(8,128)(2,1)} %get-tuple-element.8) | copy-start | bytes 491524
  172.8 112.6 %all-gather.6.cloned.1.call-start = ((), (), s32[]{:S(2)}) async-start(), calls=%async_computation.7 | async-start | bytes 18247680 | tf_op jit(solution)/shard_map/all_gather | solution.py:75
  186.6 158.8 %all-gather.8.cloned.1.call-start = ((), (), s32[]{:S(2)}) async-start(), calls=%async_computation.9 | async-start | bytes 10813440 | tf_op jit(solution)/shard_map/all_gather | solution.py:137
  187.6 193.3 %reduce-scatter.5.cloned.1.call-start = ((), (), s32[]{:S(2)}) async-start(), calls=%async_computation.8 | async-start | bytes 3276800 | tf_op jit(solution)/shard_map/reduce_scatter | solution.py:113
  300.0 45.5 %copy-start.6 = (s32[128]{0:T(128)S(1)}, s32[128]{0:T(128)}, u32[]{:S(2)}) copy-start(s32[128]{0:T(128)} %param.12) | copy-start | bytes 1540
  345.5 38.0 %copy-start.1 = (bf16[640,2560]{1,0:T(8,128)(2,1)S(1)}, bf16[640,2560]{1,0:T(8,128)(2,1)}, u32[]{:S(2)}) copy-start(bf16[640,2560]{1,0:T(8,128)(2,1)} %param.18) | copy-start | bytes 9830404
Sparse Core Ops, SparseCore 0:
  130.4 32.6 reduce-scatter.2
  172.9 35.4 all-gather.3
  210.7 74.6 all-gather.5
  288.1 57.3 all-gather.7
  347.7 33.1 reduce-scatter.4
